TPU v7x, 32 devices: a whole 2x2x4 slice. The times are simulated.
32 devices in a mesh: tm: 32 (over z, y, x, core), panel: 1.
Axes of the slice: x: 2, y: 2, z: 4, core: 2. Of those that a mesh axis runs over, the one named last changes fastest.
Arguments:
- observations: float32 [1024, 64], P('tm'), may hold values from -600 to 600
- obs_weights: float32 [1024, 64], P('tm'), may hold values from 0 to 1
- damping: float32 [1024, 256], P('tm'), may hold values from 0.1 to 1
- transition: float32 [256, 256], replicated, may hold values from -1 to 1
- obs_matrix: float32 [64, 256], replicated, may hold values from -0.25 to 0.25
- smoother_gain: float32 [256, 256], replicated, may hold values from -1 to 1
- prior_mean: float32 [256], replicated, may hold values from -6 to 6
Outputs:
- filtered: float32 [1024, 256], P('tm')
- smoothed: float32 [1024, 256], P('tm')
All inputs are finite; a program needn't handle non-finite values.
Results may differ from a plain program's by a relative error of at most 0.0003.
Values sent between devices are 32-bit elements; how exact they have to be, the bound alone decides.
A program may use at most 64 MiB of HBM per device.

v0:
```python
import jax
import jax.numpy as jnp
from jax import lax
from jax.sharding import PartitionSpec as P

highest = lax.Precision.HIGHEST


def prefix(value, axis, join, neutral, backward):
    count, mine = (lax.axis_size(axis), lax.axis_index(axis))
    pieces = jax.tree.map(lambda part: lax.all_gather(part, axis), value)
    if backward:
        pieces = jax.tree.map(lambda part: part[::-1], pieces)
        mine = count - 1 - mine
    subtotal = jax.tree.map(
        lambda part, zero: jnp.full_like(part, 0) + jnp.asarray(zero, part.dtype), value, neutral
    )

    def lap(position, subtotal):
        longer = join(subtotal, jax.tree.map(lambda part: part[position], pieces))
        return jax.tree.map(lambda new, old: jnp.where(position < mine, new, old), longer, subtotal)

    return lax.fori_loop(0, count - 1, lap, subtotal)


def product(left, right):
    return jnp.dot(left, right, precision=highest, preferred_element_type=jnp.float32)


def filter_update(estimate, obs_row, weight_row, damp_row, inject_row, transition, obs_matrix):
    predicted = product(transition, damp_row * estimate) + inject_row
    innovation = obs_row - product(obs_matrix, predicted)
    return predicted + product(weight_row * innovation, obs_matrix)


def per_device(
    observations, obs_weights, damping, transition, obs_matrix, smoother_gain, prior_mean
):
    step_count, state_width = damping.shape
    panel_count = lax.axis_size("panel")
    row_count = state_width // panel_count
    panel_index = lax.axis_index("panel")
    time_index = lax.axis_index("tm")
    block_count = lax.axis_size("tm")
    is_first = (time_index == 0).astype(jnp.float32)
    is_final = (time_index == block_count - 1).astype(jnp.float32)
    trans_t = transition.T
    obs_t = obs_matrix.T
    row_ids = lax.broadcasted_iota(jnp.int32, (row_count, state_width), 0) + panel_index * row_count
    col_ids = lax.broadcasted_iota(jnp.int32, (row_count, state_width), 1)
    start_rows = (row_ids == col_ids).astype(jnp.float32) * (1.0 - is_first)
    step_ids = lax.broadcasted_iota(jnp.int32, (step_count, 1), 0)
    inject = (step_ids == 0).astype(jnp.float32) * is_first * prior_mean[None, :]

    def forward_step(carried, inputs):
        panel_rows, estimate = carried
        obs_row, weight_row, damp_row, inject_row = inputs
        estimate = filter_update(
            estimate, obs_row, weight_row, damp_row, inject_row, transition, obs_matrix
        )
        advanced = product(panel_rows * damp_row[None, :], trans_t)
        panel_rows = advanced - product(product(advanced, obs_t) * weight_row[None, :], obs_matrix)
        return ((panel_rows, estimate), (estimate, panel_rows))

    zero_state = jnp.zeros((state_width,), jnp.float32)
    step_inputs = (observations, obs_weights, damping, inject)
    (panel_rows, block_end), trajectory = lax.scan(
        forward_step, (start_rows, zero_state), step_inputs
    )
    base_means = trajectory[0]
    summary = lax.all_gather(panel_rows, "panel", axis=0, tiled=True)
    identity = jnp.eye(state_width, dtype=jnp.float32)

    def chain_forward(inner_part, outer_part):
        return (
            product(inner_part[0], outer_part[0]),
            product(inner_part[1], outer_part[0]) + outer_part[1],
        )

    entering = prefix((summary, block_end), "tm", chain_forward, (identity, zero_state), False)[1]
    own_part = lax.dynamic_slice_in_dim(entering, panel_index * row_count, row_count)
    partial_terms = jnp.einsum("c,tcn->tn", own_part, trajectory[1], precision=highest)
    filtered = base_means + lax.psum(partial_terms, "panel")
    end_flags = (step_ids == step_count - 1).astype(jnp.float32) * is_final
    gain_powers = [smoother_gain]
    for bit_index in range(1, step_count.bit_length()):
        gain_powers.append(product(gain_powers[-1], gain_powers[-1]))
    gain_trans = product(smoother_gain, transition)
    base_smooth = filtered - (1.0 - end_flags) * product(filtered, gain_trans.T)
    for level_index in range((step_count - 1).bit_length()):
        distance = 1 << level_index
        later_rows = jnp.concatenate(
            [base_smooth[distance:], jnp.zeros((distance, state_width), jnp.float32)], axis=0
        )
        base_smooth = base_smooth + product(later_rows, gain_powers[level_index].T)
    offset = base_smooth[0]
    block_power = identity
    for bit_index in range(step_count.bit_length()):
        if step_count >> bit_index & 1:
            block_power = product(block_power, gain_powers[bit_index])

    def chain_backward(inner_part, outer_part):
        return (
            product(outer_part[0], inner_part[0]),
            product(outer_part[0], inner_part[1]) + outer_part[1],
        )

    element = (block_power * (1.0 - is_final), offset)
    incoming = prefix(element, "tm", chain_backward, (identity, zero_state), True)[1]
    lifted = product(smoother_gain, incoming)[None, :]
    for level_index in range((step_count - 1).bit_length()):
        lifted = jnp.concatenate([lifted, product(lifted, gain_powers[level_index].T)], axis=0)
    smoothed = base_smooth + jnp.flip(lifted, 0)
    return (filtered, smoothed)


def solution(mesh):
    return jax.shard_map(
        per_device,
        mesh=mesh,
        in_specs=(P("tm", None), P("tm", None), P("tm", None), P(), P(), P(), P()),
        out_specs=(P("tm", None), P("tm", None)),
        check_vma=False,
    )
```

profile of v0, /device:TPU:0, one launch (start us, length us, event | category | flops | bytes accessed | tf_op | source)
XLA Modules:
  0.0 505.2 jit_solution(17998382190177535720)
XLA Ops:
  10.1 238.2 %while.45 = (s32[]{:T(128)}, f32[256,256]{1,0:T(8,128)S(1)}, f32[256]{0:T(256)S(1)}, f32[32,256]{1,0:T(8,128)S(1)}, f32[32,256,256]{2,1,0:T(8,128)}, /*index=5*/...) while((s32[]{:T(128)}, f32[256,256]{1,0:T(8,128)S(1)}, ...), condition=%wide.region_1.2_spmd.clone, body=%wide.region_0.1_spmd.clone.sunk | while | flops 303318144 | bytes 2512819 | solution.py:67
  12.3 1.9 bitcast_dynamic-update-slice_fusion.2
  19.7 1.9 bitcast_dynamic-update-slice_fusion.2
  27.1 1.9 bitcast_dynamic-update-slice_fusion.2
  34.6 1.9 bitcast_dynamic-update-slice_fusion.2
  42.0 1.9 bitcast_dynamic-update-slice_fusion.2
  49.5 1.9 bitcast_dynamic-update-slice_fusion.2
  56.9 1.9 bitcast_dynamic-update-slice_fusion.2
  64.4 1.9 bitcast_dynamic-update-slice_fusion.2
  71.8 1.9 bitcast_dynamic-update-slice_fusion.2
  79.3 1.9 bitcast_dynamic-update-slice_fusion.2
  86.7 1.9 bitcast_dynamic-update-slice_fusion.2
  94.2 1.9 bitcast_dynamic-update-slice_fusion.2
  101.6 1.9 bitcast_dynamic-update-slice_fusion.2
  109.0 1.9 bitcast_dynamic-update-slice_fusion.2
  116.5 1.9 bitcast_dynamic-update-slice_fusion.2
  123.9 1.9 bitcast_dynamic-update-slice_fusion.2
  131.4 1.9 bitcast_dynamic-update-slice_fusion.2
  138.8 1.9 bitcast_dynamic-update-slice_fusion.2
  146.2 1.9 bitcast_dynamic-update-slice_fusion.2
  153.7 1.9 bitcast_dynamic-update-slice_fusion.2
  161.1 1.9 bitcast_dynamic-update-slice_fusion.2
  168.6 1.9 bitcast_dynamic-update-slice_fusion.2
  176.1 1.9 bitcast_dynamic-update-slice_fusion.2
  183.5 1.9 bitcast_dynamic-update-slice_fusion.2
  190.9 1.9 bitcast_dynamic-update-slice_fusion.2
  198.4 1.9 bitcast_dynamic-update-slice_fusion.2
  205.8 1.9 bitcast_dynamic-update-slice_fusion.2
  213.3 1.9 bitcast_dynamic-update-slice_fusion.2
  220.7 1.9 bitcast_dynamic-update-slice_fusion.2
  228.2 1.9 bitcast_dynamic-update-slice_fusion.2
  235.6 1.9 bitcast_dynamic-update-slice_fusion.2
  243.1 1.9 bitcast_dynamic-update-slice_fusion.2
  252.1 1.3 fusion.55
  253.5 43.7 %all-gather.3 = f32[32,1,256]{2,1,0:T(1,128)S(1)} all-gather(f32[1,1,256]{2,1,0:T(1,128)S(1)} %bitcast.183), channel_id=3, replica_groups=mesh['tm'=32,'panel'=1] {'tm'}, dimensions={0}, use_global_device_ids=true | all-gather | bytes 33792 | tf_op jit(solution)/shard_map/all_gather | solution.py:11
  297.1 31.8 %all-gather.8.cloned.1.call-done = f32[8192,256]{1,0:T(8,128)} async-done(((f32[256,256]{1,0:T(8,128)}), f32[8192,256]{1,0:T(8,128)}) %all-gather.8.cloned.1.call-update) | async-done | bytes 8388624 | tf_op jit(solution)/shard_map/all_gather | solution.py:11
  329.0 39.1 %while.46 = (s32[]{:T(128)}, f32[256]{0:T(256)S(1)}, s32[]{:T(128)}, f32[32,256,256]{2,1,0:T(8,128)}, f32[32,256]{1,0:T(8,128)S(1)}, /*index=5*/s32[]{:T(128)}, s32[]{:T(128)}) while((s32[]{:T(128)}, f32[256]{0:T(256)S(1)}, s32[]{:T(128)}, f32[32,256,256]{2,1,0:T(8,128)}, f32[32,256]{1,0:T(8,128)S(1)}, /*index=5*/s32[]{:T(128)}, ...), condition=%wide.region_3.4_spmd.clone, body=%wide.region_2.3_spmd.clone.sunk | while | flops 787460 | bytes 272498 | solution.py:23
  368.1 7.4 %fusion.54 = f32[1,32,256]{2,0,1:T(1,128)S(1)} fusion(f32[256,1,1]{0,1,2:T(1,128)S(1)} %bitcast.181, f32[32,256,256]{2,1,0:T(8,128)} %get-tuple-element.264), kind=kOutput, calls=%fused_computation.84 | convolution fusion | flops 25165824 | bytes 8422400 | tf_op jit(solution)/shard_map/c,tcn->tn/dot_general | solution.py:82
  377.7 29.7 %all-gather.10.cloned.1.call-done = f32[8192,256]{1,0:T(8,128)} async-done(((f32[256,256]{1,0:T(8,128)}), f32[8192,256]{1,0:T(8,128)}) %all-gather.10.cloned.1.call-update) | async-done | bytes 8388624 | tf_op jit(solution)/shard_map/all_gather | solution.py:11
  407.4 7.5 %rev.10 = f32[32,256,256]{2,1,0:T(8,128)} reverse(f32[32,256,256]{2,1,0:T(8,128)} %bitcast.173), dimensions={0} | reverse | bytes 16777216 | tf_op jit(solution)/shard_map/rev | solution.py:13
  414.9 39.1 %all-gather.4 = f32[32,1,256]{2,1,0:T(1,128)S(1)} all-gather(f32[1,1,256]{2,1,0:T(1,128)S(1)} %slice_bitcast_fusion), channel_id=1, replica_groups=mesh['tm'=32,'panel'=1] {'tm'}, dimensions={0}, use_global_device_ids=true | all-gather | bytes 33792 | tf_op jit(solution)/shard_map/all_gather | solution.py:11
  454.1 41.6 %while.47 = (s32[]{:T(128)}, f32[256]{0:T(256)S(1)}, s32[]{:T(128)}, f32[32,256,256]{2,1,0:T(8,128)}, f32[32,256]{1,0:T(8,128)S(1)}, /*index=5*/s32[]{:T(128)}, s32[]{:T(128)}) while((s32[]{:T(128)}, f32[256]{0:T(256)S(1)}, s32[]{:T(128)}, f32[32,256,256]{2,1,0:T(8,128)}, f32[32,256]{1,0:T(8,128)S(1)}, /*index=5*/s32[]{:T(128)}, ...), condition=%wide.region_5.6_spmd.clone, body=%wide.region_4.5_spmd.clone.sunk | while | flops 787460 | bytes 272498 | solution.py:23
  454.1 1.2 fusion.151
  455.4 1.2 fusion.151
  456.8 1.2 fusion.151
  458.1 1.2 fusion.151
  459.5 1.2 fusion.151
  460.8 1.2 fusion.151
  462.1 1.2 fusion.151
  463.5 1.2 fusion.151
  464.8 1.2 fusion.151
  466.2 1.2 fusion.151
  467.5 1.2 fusion.151
  468.9 1.2 fusion.151
  471.5 1.2 fusion.151
  474.2 1.2 fusion.151
  476.9 1.2 fusion.151
  478.2 1.2 fusion.151
  480.9 1.2 fusion.151
  483.6 1.2 fusion.151
  487.6 1.2 fusion.151
  490.3 1.2 fusion.151
  493.0 1.2 fusion.151
  494.4 1.2 fusion.151
  (631 shorter events, 236.9 us)
Async XLA Ops:
  7.2 242.0 %copy-start = (f32[256,256]{1,0:T(8,128)S(1)}, f32[256,256]{1,0:T(8,128)}, u32[]{:S(2)}) copy-start(f32[256,256]{1,0:T(8,128)} %param.18) | copy-start | bytes 786436
  7.2 321.8 %all-gather.8.cloned.1.call-start = ((), (), s32[]{:S(2)}) async-start(), calls=%async_computation | async-start | bytes 8650752 | tf_op jit(solution)/shard_map/all_gather | solution.py:11
  248.3 0.7 copy-start.1
  249.1 158.3 %all-gather.10.cloned.1.call-start = ((), (), s32[]{:S(2)}) async-start(), calls=%async_computation.1 | async-start | bytes 8650752 | tf_op jit(solution)/shard_map/all_gather | solution.py:11
  375.5 39.4 %copy-start.2 = (f32[32,256]{1,0:T(8,128)}, f32[32,256]{1,0:T(8,128)S(1)}, u32[]{:S(2)}) copy-start(f32[32,256]{1,0:T(8,128)S(1)} %bitcast_add_fusion) | copy-start | bytes 98308
Sparse Core Ops, SparseCore 0:
  249.2 79.7 all-gather.7
  331.8 75.5 all-gather.9
where the time goes:
time: 515 us; the launch traced here: 505 us
  matrix products  278 us (54%)
  blocking collectives  82.8 us (16%)
  waiting for transfers between devices  61.6 us (12%)
  local copies, waits for them, and re-layouts  59.6 us (12%)
  between operations  14.4 us (3%)
  loops' own time  5.4 us (1%)
    dot_general x273, matrix products, product(): jnp.dot(left, right, precision=highest, preferred_element_type=jnp.float32)  271 us
    all_gather x2, blocking collectives, prefix(): pieces = jax.tree.map(lambda part: lax.all_gather(part, axis), value)  82.8 us
    all_gather x2, waiting for transfers between devices, prefix(): pieces = jax.tree.map(lambda part: lax.all_gather(part, axis), value)  61.5 us
    dynamic_slice x32, local copies, waits for them, and re-layouts, per_device(): lax.scan(forward_step, (start_rows, zero_state), step_inputs)  22.6 us
    mul x32, local copies, waits for them, and re-layouts, forward_step(): product(advanced, obs_t) * weight_row[None, :]  22.3 us
  transfers between devices with their start and end apart: 2, of which 2 were waited for; matrix products, arithmetic and copies ran while one was open for 10% of the time, Pallas kernels for 0%

commit v1 on v0

v1 whole, which is shorter than its diff:
```python
import functools

import jax
import jax.numpy as jnp
from jax import lax
from jax.experimental import pallas as pl
from jax.experimental.pallas import tpu as pltpu
from jax.sharding import PartitionSpec as P

F32 = jnp.float32
BF16 = jnp.bfloat16
PAD = 8
PIECES = 4


def halves(value):
    high = value.astype(BF16)
    return high, (value - high.astype(F32)).astype(BF16)


def split_lhs(value):
    high, low = halves(value)
    return jnp.concatenate([high, low, high], axis=1)


def split_rhs(value):
    high, low = halves(value)
    return jnp.concatenate([high, high, low], axis=0)


def dot3(left, right_split):
    return jnp.dot(split_lhs(left), right_split, preferred_element_type=F32)


def exact(left, right):
    return jnp.dot(left, right, precision=lax.Precision.HIGHEST, preferred_element_type=F32)


def matvec(row, matrix):
    width = matrix.shape[1]
    column = jnp.transpose(jnp.broadcast_to(row, (128, row.shape[1])))
    parts = [
        jnp.sum(column * matrix[:, at : at + 128], axis=0, keepdims=True)
        for at in range(0, width, 128)
    ]
    return jnp.concatenate(parts, axis=1)


def kernel(
    count, y_ref, w_ref, d_ref, t_ref, h_ref, g_ref, p_ref, f_ref, s_ref,
    node, current, arrived, gpow, gsplit, tt, kt, hs, dnext, evec, uvec,
    xin, xend, chain, obuf, gath,
    mat_send, mat_recv, chain_send, chain_recv, shift_send, shift_recv, o_send, o_recv,
):
    steps, width = d_ref.shape
    depth = steps.bit_length() - 1
    span_bits = (count - 1).bit_length()
    levels = min(3, span_bits)
    window = 1 << levels
    powers = depth + span_bits
    me = lax.axis_index("tm")
    is_first = jnp.where(me == 0, 1.0, 0.0).astype(F32)
    is_final = jnp.where(me == count - 1, 1.0, 0.0).astype(F32)

    gath[...] = jnp.zeros_like(gath)
    xin[...] = jnp.zeros_like(xin)
    barrier = pltpu.get_barrier_semaphore()
    for ahead in range(1, count):
        pl.semaphore_signal(
            barrier, inc=1, device_id={"tm": lax.rem(me + ahead, count)},
            device_id_type=pl.DeviceIdType.MESH,
        )

    h = h_ref[...]
    ht = jnp.transpose(h)
    t_trans = jnp.transpose(t_ref[...])
    tt[...] = t_trans
    kt[...] = exact(t_trans, ht)
    hs[...] = split_rhs(h)
    damp = d_ref[...]
    dnext[...] = jnp.concatenate([damp[1:], jnp.ones((1, width), F32)], axis=0)
    row_ids = lax.broadcasted_iota(jnp.int32, (steps, 1), 0)
    first_row = jnp.where(row_ids == 0, 1.0, 0.0).astype(F32) * is_first
    prior = p_ref[...]
    weights = w_ref[...]
    shifted = y_ref[...] - first_row * exact(jnp.broadcast_to(prior, (8, width)), ht)[0:1]
    evec[...] = (exact(weights * shifted, h) + first_row * prior) * dnext[...]
    pad_first = lax.broadcasted_iota(jnp.int32, (PAD, width), 0) == 0

    def leaf(step, carry):
        row = pl.ds(step, 1)
        drop = dot3(kt[...] * w_ref[row, :], hs[...])
        node[step, 0:width, :] = (tt[...] - drop) * dnext[row, :]
        node[step, width:, :] = jnp.where(pad_first, evec[row, :], 0.0)
        return carry

    lax.fori_loop(0, steps, leaf, 0, unroll=2)

    def combine(left, right):
        joined = dot3(left, split_rhs(right[0:width]))
        tail = joined[width:] + right[width:]
        return joined[0:width], tail

    def join_group(first, size):
        results = [
            combine(node[2 * (first + k)], node[2 * (first + k) + 1]) for k in range(size)
        ]
        for k, (body, tail) in enumerate(results):
            node[steps + first + k, 0:width, :] = body
            node[steps + first + k, width:, :] = tail

    pairs = (steps - 2) // 2

    def join_pair(index, carry):
        join_group(2 * index, 2)
        return carry

    lax.fori_loop(0, pairs, join_pair, 0)
    join_group(steps - 2, 1)

    root = 2 * steps - 2
    damp_col = jnp.transpose(jnp.broadcast_to(damp[0:1] * (1.0 - is_first), (128, width)))
    for at in range(0, width, 128):
        current[0, 0:width, at : at + 128] = node[root, 0:width, at : at + 128] * damp_col
    current[0, width:, :] = node[root, width:, :]

    pl.semaphore_wait(barrier, count - 1)

    def square(index, carry):
        base = gpow[index]
        gpow[index + 1] = exact(base, base)
        return carry

    gpow[0] = jnp.transpose(g_ref[...])
    piece = width // PIECES
    spans = [(k * piece, piece + (PAD if k == PIECES - 1 else 0)) for k in range(PIECES)]

    def matrix_copy(level, part):
        rows = pl.ds(*spans[part])
        return pltpu.make_async_remote_copy(
            src_ref=current.at[level, rows], dst_ref=arrived.at[level, rows],
            send_sem=mat_send.at[level, part], recv_sem=mat_recv.at[level, part],
            device_id={"tm": lax.rem(me + (1 << level), count)},
            device_id_type=pl.DeviceIdType.MESH,
        )

    def send_part(level, part):
        @pl.when(me + (1 << level) < count)
        def _():
            matrix_copy(level, part).start()

    for part in range(PIECES):
        send_part(0, part)
    done = 0
    for level in range(levels):
        reach = 1 << level
        until = (powers - 1) * (level + 1) // levels
        lax.fori_loop(done, until, square, 0)
        done = until

        @pl.when(me < reach)
        def _(level=level):
            current[level + 1] = current[level]

        for part, (start, size) in enumerate(spans):

            @pl.when(me >= reach)
            def _(level=level, part=part, start=start, size=size):
                matrix_copy(level, part).wait_recv()
                joined = dot3(
                    arrived[level, start : start + size, :],
                    split_rhs(current[level, 0:width, :]),
                )
                if part < PIECES - 1:
                    current[level + 1, start : start + size, :] = joined
                else:
                    current[level + 1, start:width, :] = joined[0:piece]
                    current[level + 1, width:, :] = joined[piece:] + current[level, width:, :]

            if level + 1 < levels:
                send_part(level + 1, part)

    chain_copy = pltpu.make_async_remote_copy(
        src_ref=xend, dst_ref=chain, send_sem=chain_send, recv_sem=chain_recv,
        device_id={"tm": lax.rem(me + window, count)}, device_id_type=pl.DeviceIdType.MESH,
    )
    shift_copy = pltpu.make_async_remote_copy(
        src_ref=xend, dst_ref=xin, send_sem=shift_send, recv_sem=shift_recv,
        device_id={"tm": lax.rem(me + 1, count)}, device_id_type=pl.DeviceIdType.MESH,
    )

    def pass_on():
        @pl.when(me + window < count)
        def _():
            chain_copy.start()

        @pl.when(me + 1 < count)
        def _():
            shift_copy.start()

    @pl.when(me < window)
    def _():
        xend[...] = current[levels, width : width + 1, :]
        pass_on()

    def keep(index, carry):
        gsplit[index] = split_rhs(gpow[index])
        return carry

    lax.fori_loop(0, powers, keep, 0)

    @pl.when(me >= window)
    def _():
        chain_copy.wait_recv()
        xend[...] = (
            matvec(chain[...], current[levels, 0:width, :])
            + current[levels, width : width + 1, :]
        )
        pass_on()

    for level in range(levels):
        for part in range(PIECES):

            @pl.when(me + (1 << level) < count)
            def _(level=level, part=part):
                matrix_copy(level, part).wait_send()

    @pl.when(me + window < count)
    def _():
        chain_copy.wait_send()

    @pl.when(me >= 1)
    def _():
        shift_copy.wait_recv()

    @pl.when(me + 1 < count)
    def _():
        shift_copy.wait_send()

    uvec[0] = xin[...] * damp[0:1]
    for level in range(depth - 1, -1, -1):
        size = 1 << level
        offset = 2 * steps - (2 * steps >> level)

        def descend(index, carry, size=size, offset=offset):
            enter = uvec[2 * size * index]
            left = offset + 2 * index
            uvec[2 * size * index + size] = (
                matvec(enter, node[left, 0:width, :]) + node[left, width : width + 1, :]
            )
            return carry

        trips = steps // (2 * size)
        lax.fori_loop(0, trips, descend, 0, unroll=min(4, trips))

    before = jnp.concatenate([uvec[step] for step in range(steps)], axis=0)
    predicted = exact(before, tt[...]) + first_row * prior
    innovation = y_ref[...] - exact(predicted, ht)
    filtered = predicted + exact(weights * innovation, h)
    f_ref[...] = filtered

    last_row = jnp.where(row_ids == steps - 1, 1.0, 0.0).astype(F32) * is_final
    base = filtered - (1.0 - last_row) * exact(exact(filtered, tt[...]), gpow[0])
    for level in range(depth):
        distance = 1 << level
        later = jnp.concatenate(
            [base[distance:], jnp.zeros((distance, width), F32)], axis=0
        )
        base = base + dot3(later, gsplit[level])
    obuf[...] = base[0:1]
    copies = []
    for rank in range(count - 1):
        copy = pltpu.make_async_remote_copy(
            src_ref=obuf, dst_ref=gath.at[rank], send_sem=o_send.at[rank],
            recv_sem=o_recv.at[rank],
            device_id={"tm": lax.rem(me + 2 * count - 1 - rank, count)},
            device_id_type=pl.DeviceIdType.MESH,
        )
        copies.append(copy)

        @pl.when(me > rank)
        def _(copy=copy):
            copy.start()

    for rank, copy in enumerate(copies):

        @pl.when(me + rank + 1 < count)
        def _(copy=copy):
            copy.wait_recv()

    gathered = jnp.concatenate([gath[rank] for rank in range(gath.shape[0])], axis=0)
    for level in range(span_bits - 1, -1, -1):
        half = 1 << level
        gathered = gathered[0:half] + dot3(gathered[half:], gsplit[depth + level])
    lifted = dot3(gathered, gsplit[0])
    for level in range(depth):
        lifted = jnp.concatenate([dot3(lifted, gsplit[level]), lifted], axis=0)
    s_ref[...] = base + lifted

    for rank, copy in enumerate(copies):

        @pl.when(me > rank)
        def _(copy=copy):
            copy.wait_send()


def per_device(
    observations, obs_weights, damping, transition, obs_matrix, smoother_gain, prior_mean
):
    count = lax.axis_size("tm")
    steps, width = damping.shape
    obs = observations.shape[1]
    span_bits = (count - 1).bit_length()
    levels = min(3, span_bits)
    powers = steps.bit_length() - 1 + span_bits
    vmem = pl.BlockSpec(memory_space=pltpu.VMEM)
    out = jax.ShapeDtypeStruct((steps, width), F32)
    dma = pltpu.SemaphoreType.DMA
    return pl.pallas_call(
        functools.partial(kernel, count),
        out_shape=(out, out),
        in_specs=[vmem] * 7,
        out_specs=(vmem, vmem),
        scratch_shapes=[
            pltpu.VMEM((2 * steps - 1, width + PAD, width), F32),
            pltpu.VMEM((levels + 1, width + PAD, width), F32),
            pltpu.VMEM((levels, width + PAD, width), F32),
            pltpu.VMEM((powers, width, width), F32),
            pltpu.VMEM((powers, 3 * width, width), BF16),
            pltpu.VMEM((width, width), F32),
            pltpu.VMEM((width, obs), F32),
            pltpu.VMEM((3 * obs, width), BF16),
            pltpu.VMEM((steps, width), F32),
            pltpu.VMEM((steps, width), F32),
            pltpu.VMEM((steps, 1, width), F32),
            pltpu.VMEM((1, width), F32),
            pltpu.VMEM((1, width), F32),
            pltpu.VMEM((1, width), F32),
            pltpu.VMEM((1, width), F32),
            pltpu.VMEM((1 << span_bits, 1, width), F32),
            dma((levels, PIECES)), dma((levels, PIECES)),
            dma, dma, dma, dma,
            dma((count - 1,)), dma((count - 1,)),
        ],
        compiler_params=pltpu.CompilerParams(
            collective_id=0, has_side_effects=True, vmem_limit_bytes=56 * 1024 * 1024
        ),
    )(
        observations, obs_weights, damping, transition, obs_matrix, smoother_gain,
        prior_mean[None, :],
    )


def solution(mesh):
    return jax.shard_map(
        per_device,
        mesh=mesh,
        in_specs=(P("tm", None), P("tm", None), P("tm", None), P(), P(), P(), P()),
        out_specs=(P("tm", None), P("tm", None)),
        check_vma=False,
    )
```

time: 515 us -> 54.8 us (0.11); the launches traced: 505 us -> 54.6 us
  matrix products: 278 us -> 0 us
  blocking collectives: 82.8 us -> 0 us
  waiting for transfers between devices: 61.6 us -> 0 us
  local copies, waits for them, and re-layouts: 59.6 us -> 2 us
  Pallas kernels: 0 us -> 51.9 us
  between operations: 14.4 us -> 0.65 us
  loops' own time: 5.4 us -> 0 us
    dot_general x274 -> x0, matrix products: 278 us -> none  [the longest x273 271 us: product(): jnp.dot(left, right, precision=highest, preferred_element_type=jnp.float32)]
    all_gather x2 -> x0, blocking collectives: 82.8 us -> none  [prefix(): pieces = jax.tree.map(lambda part: lax.all_gather(part, axis), value)]
    all_gather x2 -> x0, waiting for transfers between devices: 61.5 us -> none  [prefix(): pieces = jax.tree.map(lambda part: lax.all_gather(part, axis), value)]
    pallas_call x0 -> x1, Pallas kernels: none -> 51.9 us  [per_device(): pl.pallas_call(functools.partial(kernel, count), out_shape=(out, out), in...]
    dynamic_slice x94 -> x0, local copies, waits for them, and re-layouts: 25.5 us -> none  [the longest x32 22.6 us: per_device(): lax.scan(forward_step, (start_rows, zero_state), step_inputs)]
    mul x32 -> x0, local copies, waits for them, and re-layouts: 22.3 us -> none  [forward_step(): product(advanced, obs_t) * weight_row[None, :]]
    rev x3 -> x0, local copies, waits for them, and re-layouts: 7.59 us -> none  [the longest x2 7.53 us: prefix(): pieces = jax.tree.map(lambda part: part[::-1], pieces)]
    another operation x3 -> x0, loops' own time: 5.4 us -> none  [the longest x1 2.95 us: per_device(): lax.scan(forward_step, (start_rows, zero_state), step_inputs)]
  transfers between devices with their start and end apart: 2 -> 0, of which waited for: 2 -> 0; matrix products, arithmetic and copies ran while one was open for 10% -> 0% of each run, Pallas kernels for 0% -> 0%
where the time goes in v1:
time: 54.8 us; the launch traced here: 54.6 us
  Pallas kernels  51.9 us (95%)
  local copies, waits for them, and re-layouts  2 us (4%)
  between operations  0.65 us (1%)
    pallas_call x1, Pallas kernels, per_device(): pl.pallas_call(functools.partial(kernel, count), out_shape=(out, out), in...  51.9 us
    unnamed x4, local copies, waits for them, and re-layouts  2 us

profile of v1, /device:TPU:0, one launch (start us, length us, event | category | flops | bytes accessed | tf_op | source)
XLA Modules:
  0.0 54.6 jit_solution(8382722088548590304)
XLA Ops:
  0.6 51.9 %shard_map.86 = (f32[32,256]{1,0:T(8,128)}, f32[32,256]{1,0:T(8,128)}) custom-call(f32[32,64]{1,0:T(8,128)} %y_ref.1, f32[32,64]{1,0:T(8,128)} %w_ref.1, f32[32,256]{1,0:T(8,128)} %d_ref.1, f32[256,256]{1,0:T(8,128)} %t_ref.1, f32[64,256]{1,0:T(8,128)} %h_ref.1, f32[256,256]{1,0:T(8,128)} %g_ref.1, f32[1,256]{1,0:T(1,128)} %bitcast.1), custom_call_target="tpu_custom_call" | custom-call | tf_op jit(solution)/shard_map/pallas_call | solution.py:319
  52.6 0.0 copy-start
  52.6 1.4 %copy.11 = f32[32,256]{1,0:T(8,128)} copy(f32[32,256]{1,0:T(8,128)} %get-tuple-element.4) | data formatting | bytes 65536
  54.0 0.0 copy-done
  54.0 0.6 %copy.12 = f32[32,256]{1,0:T(8,128)} copy(f32[32,256]{1,0:T(8,128)S(1)} %copy-done) | data formatting | bytes 65536
Async XLA Ops:
  52.6 1.4 %copy-start = (f32[32,256]{1,0:T(8,128)S(1)}, f32[32,256]{1,0:T(8,128)}, u32[]{:S(2)}) copy-start(f32[32,256]{1,0:T(8,128)} %get-tuple-element.5) | copy-start | bytes 98308

commit v2 on v1

--- a/solution.py
+++ b/solution.py
@@ -154,9 +154,9 @@
     done = 0
     for level in range(levels):
         reach = 1 << level
-        until = (powers - 1) * (level + 1) // levels
-        lax.fori_loop(done, until, square, 0)
-        done = until
+        if level == 0:
+            done = (powers - 1) // 2
+            lax.fori_loop(0, done, square, 0)
 
         @pl.when(me < reach)
         def _(level=level):
@@ -207,6 +207,7 @@
         gsplit[index] = split_rhs(gpow[index])
         return carry
 
+    lax.fori_loop(done, powers - 1, square, 0)
     lax.fori_loop(0, powers, keep, 0)
 
     @pl.when(me >= window)

time: 54.8 us -> 55.5 us (1.013)
  Pallas kernels: 51.9 us -> 52.7 us
    pallas_call x1, Pallas kernels: 51.9 us -> 52.7 us  [per_device(): pl.pallas_call(functools.partial(kernel, count), out_shape=(out, out), in...]
where the time goes in v2:
time: 55.5 us; the launch traced here: 55.3 us
  Pallas kernels  52.7 us (95%)
  local copies, waits for them, and re-layouts  2 us (4%)
  between operations  0.65 us (1%)
    pallas_call x1, Pallas kernels, per_device(): pl.pallas_call(functools.partial(kernel, count), out_shape=(out, out), in...  52.7 us
    unnamed x4, local copies, waits for them, and re-layouts  2 us

profile of v2, /device:TPU:0, one launch (start us, length us, event | category | flops | bytes accessed | tf_op | source)
XLA Modules:
  0.0 55.3 jit_solution(9290356281549863826)
XLA Ops:
  0.6 52.7 %shard_map.86 = (f32[32,256]{1,0:T(8,128)}, f32[32,256]{1,0:T(8,128)}) custom-call(f32[32,64]{1,0:T(8,128)} %y_ref.1, f32[32,64]{1,0:T(8,128)} %w_ref.1, f32[32,256]{1,0:T(8,128)} %d_ref.1, f32[256,256]{1,0:T(8,128)} %t_ref.1, f32[64,256]{1,0:T(8,128)} %h_ref.1, f32[256,256]{1,0:T(8,128)} %g_ref.1, f32[1,256]{1,0:T(1,128)} %bitcast.1), custom_call_target="tpu_custom_call" | custom-call | tf_op jit(solution)/shard_map/pallas_call | solution.py:320
  53.3 0.0 copy-start
  53.3 1.4 %copy.11 = f32[32,256]{1,0:T(8,128)} copy(f32[32,256]{1,0:T(8,128)} %get-tuple-element.4) | data formatting | bytes 65536
  54.7 0.0 copy-done
  54.7 0.6 %copy.12 = f32[32,256]{1,0:T(8,128)} copy(f32[32,256]{1,0:T(8,128)S(1)} %copy-done) | data formatting | bytes 65536
Async XLA Ops:
  53.3 1.4 %copy-start = (f32[32,256]{1,0:T(8,128)S(1)}, f32[32,256]{1,0:T(8,128)}, u32[]{:S(2)}) copy-start(f32[32,256]{1,0:T(8,128)} %get-tuple-element.5) | copy-start | bytes 98308
